TPU v7x, 256 devices: a whole 4x4x8 slice. The times are simulated.
256 devices in a mesh: row: 8 (over x, core), col: 32 (over y, z).
Axes of the slice: x: 4, y: 4, z: 8, core: 2. Of those that a mesh axis runs over, the one named last changes fastest.
Arguments:
- hidden: bfloat16 [4096, 8192], P('row', 'col'), may hold values from -600 to 600
- norm_gain: float32 [8192], replicated, may hold values from 0.5 to 2
- wq: bfloat16 [8192, 8192], P('row', 'col'), may hold values from -1 to 1
- wk: bfloat16 [8192, 1024], P('row', 'col'), may hold values from -1 to 1
- wv: bfloat16 [8192, 1024], P('row', 'col'), may hold values from -0.0625 to 0.0625
- wo: bfloat16 [8192, 8192], P('row', 'col'), may hold values from -0.25 to 0.25
Outputs:
- attn_out: bfloat16 [4096, 8192], P('row', 'col')
All inputs are finite; a program needn't handle non-finite values.
Results may differ from a plain program's by a relative error of at most 0.011.
Values may be sent and summed in bfloat16 or wider, within the bound.
A program may use at most 64 MiB of HBM per device.

v0:
```python
import jax
import jax.numpy as jnp
from jax import lax
from jax.sharding import PartitionSpec as P

HD = 128


def partner(array, axis, distance):
    return lax.ppermute(array, axis, [(i, i ^ 1 << distance) for i in range(lax.axis_size(axis))])


def rotary(field, positions):
    half = field.shape[-1] // 2
    steps = jnp.arange(half).astype(jnp.float32)
    freqs = 10000.0 ** (-steps / half)
    angles = positions.astype(jnp.float32)[:, None] * freqs[None, :]
    cosine = jnp.cos(angles)[:, None, :]
    sine = jnp.sin(angles)[:, None, :]
    first = field[..., :half]
    second = field[..., half:]
    return jnp.concatenate(
        [first * cosine - second * sine, second * cosine + first * sine], axis=-1
    )


def order_pair(mine, other, col_index, bit, axis_dim):
    upper = col_index // 2**bit % 2 == 1
    lower_part = jnp.where(upper, other, mine)
    upper_part = jnp.where(upper, mine, other)
    return jnp.concatenate([lower_part, upper_part], axis=axis_dim)


def per_device(hidden, norm_gain, wq, wk, wv, wo):
    tok_rows = hidden.shape[0]
    panel = lax.all_gather(hidden, "col", axis=1, tiled=True)
    values_in = panel.astype(jnp.float32)
    meansq = jnp.mean(values_in * values_in, axis=1, keepdims=True)
    normed = (values_in * lax.rsqrt(meansq + 1e-05) * norm_gain).astype(jnp.bfloat16)
    kv_cols = wk.shape[1]
    group = max(1, HD // kv_cols)
    bits = group.bit_length() - 1
    col_index = lax.axis_index("col")
    stacked = jnp.stack((wk, wv), axis=1)
    for bit in range(bits):
        other = partner(stacked, "col", bit)
        stacked = order_pair(stacked, other, col_index, bit, 2)
    columns = normed
    query_part = jnp.dot(
        columns, lax.all_gather(wq, "row", axis=0, tiled=True), preferred_element_type=jnp.float32
    )
    pair_part = jnp.einsum(
        "ho,omr->hmr",
        columns,
        lax.all_gather(stacked, "row", axis=0, tiled=True),
        preferred_element_type=jnp.float32,
    )
    heads_here = wq.shape[1] // HD
    kv_here = pair_part.shape[2] // HD
    per_kv = heads_here // kv_here
    positions = lax.axis_index("row") * tok_rows + jnp.arange(tok_rows)
    queries = rotary(query_part.reshape(tok_rows, heads_here, HD), positions).astype(jnp.bfloat16)
    queries = queries.reshape(tok_rows, kv_here, per_kv, HD)
    keys = rotary(pair_part[:, 0].reshape(tok_rows, kv_here, HD), positions).astype(jnp.bfloat16)
    values = pair_part[:, 1].reshape(tok_rows, kv_here, HD).astype(jnp.bfloat16)
    scale = HD ** (-0.5)
    best = jnp.full((kv_here, per_kv, tok_rows), -1e30, jnp.float32)
    key_piece = lax.all_gather(keys, "row", axis=0, tiled=True)
    value_piece = lax.all_gather(values, "row", axis=0, tiled=True)
    count = key_piece.shape[0]
    scores = (
        jnp.einsum("tagd,nad->agtn", queries, key_piece, preferred_element_type=jnp.float32) * scale
    )
    key_pos = jnp.arange(count)
    visible = positions[:, None] >= key_pos[None, :]
    scores = jnp.where(visible, scores, -jnp.inf)
    fresh = jnp.maximum(best, jnp.max(scores, axis=3))
    probs = jnp.exp(scores - fresh[..., None])
    total = jnp.sum(probs, axis=3)
    update = jnp.einsum(
        "agtn,nad->agtd",
        probs.astype(jnp.bfloat16),
        value_piece,
        preferred_element_type=jnp.float32,
    )
    numer = update
    best, total, numer = (fresh, total, numer)
    heads = (
        (numer / total[..., None])
        .transpose(2, 0, 1, 3)
        .reshape(tok_rows, heads_here * HD)
        .astype(jnp.bfloat16)
    )
    head_panel = lax.all_gather(heads, "col", axis=1, tiled=True)
    columns = head_panel
    result = jnp.dot(
        columns, lax.all_gather(wo, "row", axis=0, tiled=True), preferred_element_type=jnp.float32
    )
    return result.astype(jnp.bfloat16)


def solution(mesh):
    in_specs = (
        P("row", "col"),
        P(),
        P("row", "col"),
        P("row", "col"),
        P("row", "col"),
        P("row", "col"),
    )
    out_specs = P("row", "col")
    return jax.shard_map(
        per_device, mesh=mesh, in_specs=in_specs, out_specs=out_specs, check_vma=False
    )
```

profile of v0, /device:TPU:1, one launch (start us, length us, event | category | flops | bytes accessed | tf_op | source)
XLA Modules:
  0.0 396.9 jit_solution(9538606364416327431)
XLA Ops:
  7.3 0.9 pad_maximum_fusion.2
  8.2 2.6 collective-permute-start
  10.7 2.4 collective-permute-done
  13.1 0.9 broadcast_select_fusion.3
  14.0 3.8 collective-permute-start.1
  17.9 11.3 %collective-permute-done.1 = bf16[1024,2,64]{0,2,1:T(8,128)(2,1)S(1)} collective-permute-done((bf16[1024,2,64]{0,2,1:T(8,128)(2,1)S(1)}, bf16[1024,2,64]{0,2,1:T(8,128)(2,1)S(1)}, u32[]{:S(2)}, u32[]{:S(2)}) %collective-permute-start.1) | collective-permute-done | bytes 262176 | tf_op jit(solution)/shard_map/ppermute | solution.py:10
  31.0 86.2 %all-gather.8.cloned.1.call-done = bf16[512,8192]{1,0:T(8,128)(2,1)} async-done(((bf16[512,256]{1,0:T(8,128)(2,1)}), bf16[512,8192]{1,0:T(8,128)(2,1)}) %all-gather.8.cloned.1.call-update) | async-done | bytes 8388624 | tf_op jit(solution)/shard_map/all_gather | solution.py:36
  117.1 5.1 %fusion = f32[512]{0:T(512)S(1)} fusion(bf16[512,8192]{1,0:T(8,128)(2,1)} %all-gather.8.cloned.1.call-done), kind=kLoop, calls=%fused_computation.2 | loop fusion | flops 12582400 | bytes 8390656 | tf_op jit(solution)/shard_map/reduce_sum | solution.py:38
  122.3 31.8 %all-gather.10.cloned.1.call-done = bf16[8192,2,128]{0,2,1:T(8,128)(2,1)} async-done(((bf16[1024,2,128]{0,2,1:T(8,128)(2,1)}), bf16[8192,2,128]{0,2,1:T(8,128)(2,1)}) %all-gather.10.cloned.1.call-update) | async-done | bytes 4194320 | tf_op jit(solution)/shard_map/all_gather | solution.py:55
  154.1 7.0 %fusion.12 = f32[512,256]{0,1:S(1)} fusion(bf16[8192,256]{0,1:T(8,128)(2,1)} %bitcast.61, bf16[512,8192]{1,0:T(8,128)(2,1)} %all-gather.8.cloned.1.call-done, f32[8192]{0:T(1024)S(1)} %copy-done.1, f32[512]{0:T(512)S(1)} %add_rsqrt_fusion), kind=kOutput, calls=%fused_computation.15 | convolution fusion | flops 2164260864 | bytes 13142016
  163.9 1.8 multiply_cosine_fusion
  165.7 1.7 iota_compare_fusion
  167.5 23.2 %all-gather.14.cloned.1.call-done = bf16[8192,256]{1,0:T(8,128)(2,1)} async-done(((bf16[1024,256]{1,0:T(8,128)(2,1)}), bf16[8192,256]{1,0:T(8,128)(2,1)}) %all-gather.14.cloned.1.call-update) | async-done | bytes 4194320 | tf_op jit(solution)/shard_map/all_gather | solution.py:50
  190.6 7.6 %fusion.10 = f32[512,256]{0,1:T(8,128)S(1)} fusion(bf16[8192,256]{1,0:T(8,128)(2,1)} %all-gather.14.cloned.1.call-done, bf16[512,8192]{1,0:T(8,128)(2,1)} %all-gather.8.cloned.1.call-done, f32[8192]{0:T(1024)S(1)} %copy-done.1, f32[512]{0:T(512)S(1)} %add_rsqrt_fusion), kind=kOutput, calls=%fused_computation.14 | convolution fusion | flops 2164260864 | bytes 13142016 | tf_op jit(solution)/shard_map/dot_general | solution.py:49
  198.7 1.9 subtract_convert_fusion
  200.5 17.7 %all-gather.12.cloned.1.call-done = bf16[4096,1,128]{0,2,1:T(8,128)(2,1)} async-done(((bf16[512,1,128]{0,2,1:T(8,128)(2,1)}), bf16[4096,1,128]{0,2,1:T(8,128)(2,1)}) %all-gather.12.cloned.1.call-update) | async-done | bytes 1048592 | tf_op jit(solution)/shard_map/all_gather | solution.py:68
  218.2 5.1 %fusion.5 = (f32[2,512]{1,0:T(2,128)S(1)}, f32[4096,512,2]{1,0,2:T(8,128)S(1)}) fusion(pred[512,4096]{0,1:T(8,128)(4,1)S(1)} %iota_compare_fusion, bf16[512,2,64]{2,0,1:T(8,128)(2,1)} %get-tuple-element.6, bf16[512,2,64]{2,0,1:T(8,128)(2,1)S(1)} %get-tuple-element.5, bf16[4096,1,128]{0,2,1:T(8,128)(2,1)} %all-gather.12.cloned.1.call-done), kind=kOutput, calls=%fused_computation.9 | convolution fusion | flops 1086848000 | bytes 20189184 | tf_op jit(solution)/shard_map/tagd,nad->agtn/dot_general | solution.py:72
  223.3 5.7 %copy-done = f32[4096,512,2]{1,0,2:T(8,128)} copy-done((f32[4096,512,2]{1,0,2:T(8,128)}, f32[4096,512,2]{1,0,2:T(8,128)S(1)}, u32[]{:S(2)}) %copy-start) | copy-done | bytes 16777240
  229.0 4.2 %fusion.3 = f32[2,512]{1,0:T(2,128)S(1)} fusion(f32[4096,512,2]{1,0,2:T(8,128)S(1)} %get-tuple-element.18, f32[2,512]{1,0:T(2,128)S(1)} %broadcast_maximum_fusion, pred[512,4096]{0,1:T(8,128)(4,1)S(1)} %iota_compare_fusion), kind=kLoop, calls=%fused_computation.7 | loop fusion | flops 16776192 | bytes 18882560 | tf_op jit(solution)/shard_map/reduce_sum | solution.py:79
  233.2 12.6 %all-gather.16.cloned.1.call-done = bf16[4096,1,128]{0,2,1:T(8,128)(2,1)} async-done(((bf16[512,1,128]{0,2,1:T(8,128)(2,1)}), bf16[4096,1,128]{0,2,1:T(8,128)(2,1)}) %all-gather.16.cloned.1.call-update) | async-done | bytes 1048592 | tf_op jit(solution)/shard_map/all_gather | solution.py:69
  245.8 11.7 %fusion.22 = bf16[2,512,128]{1,2,0:T(8,128)(2,1)} fusion(f32[4096,512,2]{1,0,2:T(8,128)} %copy-done, f32[2,512]{1,0:T(2,128)S(1)} %broadcast_maximum_fusion, pred[512,4096]{0,1:T(8,128)(4,1)S(1)} %iota_compare_fusion, bf16[4096,1,128]{0,2,1:T(8,128)(2,1)} %all-gather.16.cloned.1.call-done, f32[2,512]{1,0:T(2,128)S(1)} %fusion.3), kind=kOutput, calls=%fused_computation.21 | convolution fusion | flops 1090781184 | bytes 20193280 | tf_op jit(solution)/shard_map/agtn,nad->agtd/dot_general | solution.py:80
  257.4 24.6 %all-gather.20.cloned.1.call-done = bf16[8192,256]{1,0:T(8,128)(2,1)} async-done(((bf16[1024,256]{1,0:T(8,128)(2,1)}), bf16[8192,256]{1,0:T(8,128)(2,1)}) %all-gather.20.cloned.1.call-update) | async-done | bytes 4194320 | tf_op jit(solution)/shard_map/all_gather | solution.py:97
  282.0 100.3 %all-gather.18.cloned.1.call-done = bf16[512,8192]{0,1:T(8,128)(2,1)} async-done(((bf16[512,256]{0,1:T(8,128)(2,1)}), bf16[512,8192]{0,1:T(8,128)(2,1)}) %all-gather.18.cloned.1.call-update) | async-done | bytes 8388624 | tf_op jit(solution)/shard_map/all_gather | solution.py:94
  382.4 7.7 %convolution_convert_fusion = bf16[512,256]{1,0:T(8,128)(2,1)} fusion(bf16[512,8192]{0,1:T(8,128)(2,1)} %all-gather.18.cloned.1.call-done, bf16[8192,256]{1,0:T(8,128)(2,1)} %all-gather.20.cloned.1.call-done), kind=kOutput, calls=%fused_computation.16 | convolution fusion | flops 2147614720 | bytes 12845056 | tf_op jit(solution)/shard_map/dot_general | solution.py:96
  (31 shorter events, 5.7 us)
Async XLA Ops:
  6.5 147.6 %copy-start.1 = (f32[8192]{0:T(1024)S(1)}, f32[8192]{0:T(1024)}, u32[]{:S(2)}) copy-start(f32[8192]{0:T(1024)} %param.7) | copy-start | bytes 98308
  6.5 110.6 %all-gather.8.cloned.1.call-start = ((), (), s32[]{:S(2)}) async-start(), calls=%async_computation | async-start | bytes 8650752 | tf_op jit(solution)/shard_map/all_gather | solution.py:36
  7.3 146.8 %all-gather.10.cloned.1.call-start = ((), (), s32[]{:S(2)}) async-start(), calls=%async_computation.1 | async-start | bytes 4718592 | tf_op jit(solution)/shard_map/all_gather | solution.py:55
  8.2 4.9 %collective-permute-start = (bf16[1024,2,32]{0,2,1:T(8,128)(2,1)S(1)}, bf16[1024,2,32]{0,2,1:T(8,128)(2,1)S(1)}, u32[]{:S(2)}, u32[]{:S(2)}) collective-permute-start(bf16[1024,2,32]{0,2,1:T(8,128)(2,1)S(1)} %pad_maximum_fusion.2), channel_id=1, source_target_pairs={{0,1},{1,0},{2,3},{3,2},{4,5},{5,4},{6,7},{7,6},{8,9},{9,8},{10,11... | collective-permute-start | bytes 393224 | tf_op jit(solution)/shard_map/ppermute | solution.py:10
  14.0 15.2 %collective-permute-start.1 = (bf16[1024,2,64]{0,2,1:T(8,128)(2,1)S(1)}, bf16[1024,2,64]{0,2,1:T(8,128)(2,1)S(1)}, u32[]{:S(2)}, u32[]{:S(2)}) collective-permute-start(bf16[1024,2,64]{0,2,1:T(8,128)(2,1)S(1)} %pad_maximum_fusion.1), channel_id=1, source_target_pairs={{0,2},{1,3},{2,0},{3,1},{4,6},{5,7},{6,4},{7,5},{8,10},{9,11},{10,... | collective-permute-start | bytes 786440 | tf_op jit(solution)/shard_map/ppermute | solution.py:10
  30.2 160.5 %all-gather.14.cloned.1.call-start = ((), (), s32[]{:S(2)}) async-start(), calls=%async_computation.3 | async-start | bytes 4718592 | tf_op jit(solution)/shard_map/all_gather | solution.py:50
  30.9 187.3 %all-gather.12.cloned.1.call-start = ((), (), s32[]{:S(2)}) async-start(), calls=%async_computation.2 | async-start | bytes 1179648 | tf_op jit(solution)/shard_map/all_gather | solution.py:68
  162.4 83.4 %all-gather.16.cloned.1.call-start = ((), (), s32[]{:S(2)}) async-start(), calls=%async_computation.4 | async-start | bytes 1179648 | tf_op jit(solution)/shard_map/all_gather | solution.py:69
  163.1 118.9 %all-gather.20.cloned.1.call-start = ((), (), s32[]{:S(2)}) async-start(), calls=%async_computation.6 | async-start | bytes 4718592 | tf_op jit(solution)/shard_map/all_gather | solution.py:97
  163.7 218.7 %all-gather.18.cloned.1.call-start = ((), (), s32[]{:S(2)}) async-start(), calls=%async_computation.5 | async-start | bytes 8650752 | tf_op jit(solution)/shard_map/all_gather | solution.py:94
  223.3 5.7 %copy-start = (f32[4096,512,2]{1,0,2:T(8,128)}, f32[4096,512,2]{1,0,2:T(8,128)S(1)}, u32[]{:S(2)}) copy-start(f32[4096,512,2]{1,0,2:T(8,128)S(1)} %get-tuple-element.18) | copy-start | bytes 50331652
Sparse Core Ops, SparseCore 0:
  9.8 107.2 all-gather.7
  119.0 35.0 all-gather.9
  156.0 34.6 all-gather.13
  192.3 25.8 all-gather.11
  219.9 25.7 all-gather.15
  247.5 34.5 all-gather.19
  284.6 97.6 all-gather.17
where the time goes:
time: 397 us
  waiting for transfers between devices  312 us (79%)
  matrix products  39 us (10%)
  other arithmetic  18.7 us (5%)
  between operations  13.6 us (3%)
  local copies, waits for them, and re-layouts  6.8 us (2%)
  starting transfers between devices  6.8 us (2%)
    all_gather x1, waiting for transfers between devices, per_device(): head_panel = lax.all_gather(heads, 'col', axis=1, tiled=True)  100 us
    all_gather x1, waiting for transfers between devices, per_device(): panel = lax.all_gather(hidden, 'col', axis=1, tiled=True)  86.2 us
    all_gather x1, waiting for transfers between devices, per_device(): lax.all_gather(stacked, 'row', axis=0, tiled=True)  31.8 us
    all_gather x1, waiting for transfers between devices, per_device(): lax.all_gather(wo, 'row', axis=0, tiled=True)  24.6 us
    all_gather x1, waiting for transfers between devices, per_device(): lax.all_gather(wq, 'row', axis=0, tiled=True)  23.2 us
    all_gather x1, waiting for transfers between devices, per_device(): key_piece = lax.all_gather(keys, 'row', axis=0, tiled=True)  17.7 us
    ppermute x2, waiting for transfers between devices, partner(): lax.ppermute(array, axis, [(i, i ^ 1 << distance) for i in range(lax.axis...  13.7 us
    all_gather x1, waiting for transfers between devices, per_device(): value_piece = lax.all_gather(values, 'row', axis=0, tiled=True)  12.6 us
  transfers between devices with their start and end apart: 9, of which 9 were waited for; matrix products, arithmetic and copies ran while one was open for 13% of the time, Pallas kernels for 0%

commit v1 on v0

--- a/solution.py
+++ b/solution.py
@@ -49,12 +49,22 @@
     query_part = jnp.dot(
         columns, lax.all_gather(wq, "row", axis=0, tiled=True), preferred_element_type=jnp.float32
     )
-    pair_part = jnp.einsum(
-        "ho,omr->hmr",
-        columns,
-        lax.all_gather(stacked, "row", axis=0, tiled=True),
-        preferred_element_type=jnp.float32,
-    )
+    size, index, extent = (lax.axis_size("row"), lax.axis_index("row"), stacked.shape[0])
+    right = [(i_2, (i_2 + 1) % size) for i_2 in range(size)]
+    block, total_2 = (stacked, None)
+    for step in range(size):
+        coming = lax.ppermute(block, "row", right) if step < size - 1 else None
+        update_2 = jnp.einsum(
+            "ho,omr->hmr",
+            lax.dynamic_slice_in_dim(
+                columns, (index - step) % size * extent, block.shape[0], axis=1
+            ),
+            block,
+            preferred_element_type=jnp.float32,
+        )
+        total_2 = update_2 if total_2 is None else total_2 + update_2
+        block = coming
+    pair_part = total_2
     heads_here = wq.shape[1] // HD
     kv_here = pair_part.shape[2] // HD
     per_kv = heads_here // kv_here

time: 397 us -> 361 us (0.909)
  waiting for transfers between devices: 312 us -> 245 us
  starting transfers between devices: 6.8 us -> 24.3 us
  other arithmetic: 18.7 us -> 28.3 us
    all_gather x1, waiting for transfers between devices: 86.2 us -> 33.1 us  [per_device(): panel = lax.all_gather(hidden, 'col', axis=1, tiled=True)]
    ppermute x0 -> x7, waiting for transfers between devices: none -> 37.1 us  [per_device(): coming = lax.ppermute(block, 'row', right) if step < size - 1 else None]
    all_gather x1 -> x0, waiting for transfers between devices: 31.8 us -> none  [per_device(): lax.all_gather(stacked, 'row', axis=0, tiled=True)]
    all_gather x1, waiting for transfers between devices: 23.2 us -> 4.24 us  [per_device(): lax.all_gather(wq, 'row', axis=0, tiled=True)]
    ppermute x0 -> x7, starting transfers between devices: none -> 17.5 us  [per_device(): coming = lax.ppermute(block, 'row', right) if step < size - 1 else None]
    convert_element_type x0 -> x1, other arithmetic: none -> 9.97 us  [per_device(): (values_in * lax.rsqrt(meansq + 1e-05) * norm_gain).astype(jnp.bfloat16)]
    unnamed x1 -> x8, matrix products: 7.02 us -> 10.7 us
  transfers between devices with their start and end apart: 9 -> 15, of which waited for: 9 -> 14; matrix products, arithmetic and copies ran while one was open for 13% -> 18% of each run, Pallas kernels for 0% -> 0%
where the time goes in v1:
time: 361 us; the launch traced here: 360 us
  waiting for transfers between devices  245 us (68%)
  matrix products  42 us (12%)
  other arithmetic  28.3 us (8%)
  starting transfers between devices  24.3 us (7%)
  between operations  13.7 us (4%)
  local copies, waits for them, and re-layouts  6.82 us (2%)
    all_gather x1, waiting for transfers between devices, per_device(): head_panel = lax.all_gather(heads, 'col', axis=1, tiled=True)  100 us
    ppermute x7, waiting for transfers between devices, per_device(): coming = lax.ppermute(block, 'row', right) if step < size - 1 else None  37.1 us
    all_gather x1, waiting for transfers between devices, per_device(): panel = lax.all_gather(hidden, 'col', axis=1, tiled=True)  33.1 us
    all_gather x1, waiting for transfers between devices, per_device(): lax.all_gather(wo, 'row', axis=0, tiled=True)  24.6 us
    all_gather x1, waiting for transfers between devices, per_device(): key_piece = lax.all_gather(keys, 'row', axis=0, tiled=True)  18.5 us
    ppermute x7, starting transfers between devices, per_device(): coming = lax.ppermute(block, 'row', right) if step < size - 1 else None  17.5 us
    ppermute x2, waiting for transfers between devices, partner(): lax.ppermute(array, axis, [(i, i ^ 1 << distance) for i in range(lax.axis...  13.7 us
    all_gather x1, waiting for transfers between devices, per_device(): value_piece = lax.all_gather(values, 'row', axis=0, tiled=True)  12.6 us
  transfers between devices with their start and end apart: 15, of which 14 were waited for; matrix products, arithmetic and copies ran while one was open for 18% of the time, Pallas kernels for 0%

profile of v1, /device:TPU:1, one launch (start us, length us, event | category | flops | bytes accessed | tf_op | source)
XLA Modules:
  0.0 360.3 jit_solution(18051121846124449026)
XLA Ops:
  14.0 3.8 %collective-permute-start.1 = (bf16[1024,2,64]{0,2,1:T(8,128)(2,1)S(1)}, bf16[1024,2,64]{0,2,1:T(8,128)(2,1)S(1)}, u32[]{:S(2)}, u32[]{:S(2)}) collective-permute-start(bf16[1024,2,64]{0,2,1:T(8,128)(2,1)S(1)} %pad_maximum_fusion.1), channel_id=1, source_target_pairs={{0,2},{1,3},{2,0},{3,1},{4,6},{5,7},{6,4},{7,5},{8,10},{9,11},{10,... | collective-permute-start | bytes 786440 | tf_op jit(solution)/shard_map/ppermute | solution.py:10
  17.9 11.3 %collective-permute-done.1 = bf16[1024,2,64]{0,2,1:T(8,128)(2,1)S(1)} collective-permute-done((bf16[1024,2,64]{0,2,1:T(8,128)(2,1)S(1)}, bf16[1024,2,64]{0,2,1:T(8,128)(2,1)S(1)}, u32[]{:S(2)}, u32[]{:S(2)}) %collective-permute-start.1) | collective-permute-done | bytes 262176 | tf_op jit(solution)/shard_map/ppermute | solution.py:10
  29.4 2.8 collective-permute-start.2
  32.1 6.1 %collective-permute-done.2 = bf16[1024,2,128]{0,2,1:T(8,128)(2,1)S(1)} collective-permute-done((bf16[1024,2,128]{0,2,1:T(8,128)(2,1)S(1)}, bf16[1024,2,128]{0,2,1:T(8,128)(2,1)S(1)}, u32[]{:S(2)}, u32[]{:S(2)}) %collective-permute-start.2) | collective-permute-done | bytes 524320 | tf_op jit(solution)/shard_map/ppermute | solution.py:56
  40.7 6.1 %collective-permute-done.3 = bf16[1024,2,128]{0,2,1:T(8,128)(2,1)S(1)} collective-permute-done((bf16[1024,2,128]{0,2,1:T(8,128)(2,1)S(1)}, bf16[1024,2,128]{0,2,1:T(8,128)(2,1)S(1)}, u32[]{:S(2)}, u32[]{:S(2)}) %collective-permute-start.3) | collective-permute-done | bytes 524320 | tf_op jit(solution)/shard_map/ppermute | solution.py:56
  49.4 6.1 %collective-permute-done.4 = bf16[1024,2,128]{0,2,1:T(8,128)(2,1)S(1)} collective-permute-done((bf16[1024,2,128]{0,2,1:T(8,128)(2,1)S(1)}, bf16[1024,2,128]{0,2,1:T(8,128)(2,1)S(1)}, u32[]{:S(2)}, u32[]{:S(2)}) %collective-permute-start.4) | collective-permute-done | bytes 524320 | tf_op jit(solution)/shard_map/ppermute | solution.py:56
  57.9 6.1 %collective-permute-done.5 = bf16[1024,2,128]{0,2,1:T(8,128)(2,1)S(1)} collective-permute-done((bf16[1024,2,128]{0,2,1:T(8,128)(2,1)S(1)}, bf16[1024,2,128]{0,2,1:T(8,128)(2,1)S(1)}, u32[]{:S(2)}, u32[]{:S(2)}) %collective-permute-start.5) | collective-permute-done | bytes 524320 | tf_op jit(solution)/shard_map/ppermute | solution.py:56
  66.5 6.1 %collective-permute-done.6 = bf16[1024,2,128]{0,2,1:T(8,128)(2,1)} collective-permute-done((bf16[1024,2,128]{0,2,1:T(8,128)(2,1)S(1)}, bf16[1024,2,128]{0,2,1:T(8,128)(2,1)}, u32[]{:S(2)}, u32[]{:S(2)}) %collective-permute-start.6) | collective-permute-done | bytes 524320 | tf_op jit(solution)/shard_map/ppermute | solution.py:56
  72.7 2.6 collective-permute-start.7
  75.3 6.6 %collective-permute-done.7 = bf16[1024,2,128]{0,2,1:T(8,128)(2,1)S(1)} collective-permute-done((bf16[1024,2,128]{0,2,1:T(8,128)(2,1)}, bf16[1024,2,128]{0,2,1:T(8,128)(2,1)S(1)}, u32[]{:S(2)}, u32[]{:S(2)}) %collective-permute-start.7) | collective-permute-done | bytes 524320 | tf_op jit(solution)/shard_map/ppermute | solution.py:56
  84.1 33.1 %all-gather.7.cloned.1.call-done = bf16[512,8192]{1,0:T(8,128)(2,1)} async-done(((bf16[512,256]{1,0:T(8,128)(2,1)}), bf16[512,8192]{1,0:T(8,128)(2,1)}) %all-gather.7.cloned.1.call-update) | async-done | bytes 8388624 | tf_op jit(solution)/shard_map/all_gather | solution.py:36
  117.1 5.1 %fusion = f32[512]{0:T(512)S(1)} fusion(bf16[512,8192]{1,0:T(8,128)(2,1)} %all-gather.7.cloned.1.call-done), kind=kLoop, calls=%fused_computation.2 | loop fusion | flops 12582400 | bytes 8390656 | tf_op jit(solution)/shard_map/reduce_sum | solution.py:38
  122.2 10.0 %fusion.2 = bf16[512,8192]{1,0:T(8,128)(2,1)} fusion(bf16[512,8192]{1,0:T(8,128)(2,1)} %all-gather.7.cloned.1.call-done, f32[8192]{0:T(1024)S(1)} %copy-done.2, f32[512]{0:T(512)S(1)} %add_rsqrt_fusion), kind=kLoop, calls=%fused_computation.4 | loop fusion | flops 16777216 | bytes 16812032 | tf_op jit(solution)/shard_map/convert_element_type | solution.py:39
  149.9 4.2 %all-gather.11.cloned.1.call-done = bf16[8192,256]{1,0:T(8,128)(2,1)} async-done(((bf16[1024,256]{1,0:T(8,128)(2,1)}), bf16[8192,256]{1,0:T(8,128)(2,1)}) %all-gather.11.cloned.1.call-update) | async-done | bytes 4194320 | tf_op jit(solution)/shard_map/all_gather | solution.py:50
  154.1 6.9 %fusion.63 = f32[512,256]{0,1:T(8,128)S(1)} fusion(bf16[512,8192]{1,0:T(8,128)(2,1)} %fusion.2, bf16[8192,256]{1,0:T(8,128)(2,1)} %all-gather.11.cloned.1.call-done), kind=kOutput, calls=%fused_computation.80 | convolution fusion | flops 2147483648 | bytes 13107200 | tf_op jit(solution)/shard_map/dot_general | solution.py:49
  163.4 18.5 %all-gather.9.cloned.1.call-done = bf16[4096,1,128]{0,2,1:T(8,128)(2,1)} async-done(((bf16[512,1,128]{0,2,1:T(8,128)(2,1)}), bf16[4096,1,128]{0,2,1:T(8,128)(2,1)}) %all-gather.9.cloned.1.call-update) | async-done | bytes 1048592 | tf_op jit(solution)/shard_map/all_gather | solution.py:78
  181.9 5.1 %fusion.5 = (f32[2,512]{1,0:T(2,128)S(1)}, f32[4096,512,2]{1,0,2:T(8,128)S(1)}) fusion(pred[512,4096]{0,1:T(8,128)(4,1)S(1)} %iota_compare_fusion, bf16[512,2,64]{2,0,1:T(8,128)(2,1)} %get-tuple-element.6, bf16[512,2,64]{2,0,1:T(8,128)(2,1)S(1)} %get-tuple-element.5, bf16[4096,1,128]{0,2,1:T(8,128)(2,1)} %all-gather.9.cloned.1.call-done), kind=kOutput, calls=%fused_computation.9 | convolution fusion | flops 1086848000 | bytes 20189184 | tf_op jit(solution)/shard_map/tagd,nad->agtn/dot_general | solution.py:82
  187.0 5.7 %copy-done.1 = f32[4096,512,2]{1,0,2:T(8,128)} copy-done((f32[4096,512,2]{1,0,2:T(8,128)}, f32[4096,512,2]{1,0,2:T(8,128)S(1)}, u32[]{:S(2)}) %copy-start.1) | copy-done | bytes 16777240
  192.7 4.2 %fusion.3 = f32[2,512]{1,0:T(2,128)S(1)} fusion(f32[4096,512,2]{1,0,2:T(8,128)S(1)} %get-tuple-element.18, f32[2,512]{1,0:T(2,128)S(1)} %broadcast_maximum_fusion, pred[512,4096]{0,1:T(8,128)(4,1)S(1)} %iota_compare_fusion), kind=kLoop, calls=%fused_computation.7 | loop fusion | flops 16776192 | bytes 18882560 | tf_op jit(solution)/shard_map/reduce_sum | solution.py:89
  196.8 12.6 %all-gather.13.cloned.1.call-done = bf16[4096,1,128]{0,2,1:T(8,128)(2,1)} async-done(((bf16[512,1,128]{0,2,1:T(8,128)(2,1)}), bf16[4096,1,128]{0,2,1:T(8,128)(2,1)}) %all-gather.13.cloned.1.call-update) | async-done | bytes 1048592 | tf_op jit(solution)/shard_map/all_gather | solution.py:79
  209.4 11.7 %fusion.34 = bf16[2,512,128]{1,2,0:T(8,128)(2,1)} fusion(f32[4096,512,2]{1,0,2:T(8,128)} %copy-done.1, f32[2,512]{1,0:T(2,128)S(1)} %broadcast_maximum_fusion, pred[512,4096]{0,1:T(8,128)(4,1)S(1)} %iota_compare_fusion, bf16[4096,1,128]{0,2,1:T(8,128)(2,1)} %all-gather.13.cloned.1.call-done, f32[2,512]{1,0:T(2,128)S(1)} %fusion.3), kind=kOutput, calls=%fused_computation.35 | convolution fusion | flops 1090781184 | bytes 20193280 | tf_op jit(solution)/shard_map/agtn,nad->agtd/dot_general | solution.py:90
  221.1 24.6 %all-gather.17.cloned.1.call-done = bf16[8192,256]{1,0:T(8,128)(2,1)} async-done(((bf16[1024,256]{1,0:T(8,128)(2,1)}), bf16[8192,256]{1,0:T(8,128)(2,1)}) %all-gather.17.cloned.1.call-update) | async-done | bytes 4194320 | tf_op jit(solution)/shard_map/all_gather | solution.py:107
  245.7 100.2 %all-gather.15.cloned.1.call-done = bf16[512,8192]{0,1:T(8,128)(2,1)} async-done(((bf16[512,256]{0,1:T(8,128)(2,1)}), bf16[512,8192]{0,1:T(8,128)(2,1)}) %all-gather.15.cloned.1.call-update) | async-done | bytes 8388624 | tf_op jit(solution)/shard_map/all_gather | solution.py:104
  345.8 7.7 %convolution_convert_fusion = bf16[512,256]{1,0:T(8,128)(2,1)} fusion(bf16[512,8192]{0,1:T(8,128)(2,1)} %all-gather.15.cloned.1.call-done, bf16[8192,256]{1,0:T(8,128)(2,1)} %all-gather.17.cloned.1.call-done), kind=kOutput, calls=%fused_computation.14 | convolution fusion | flops 2147614720 | bytes 12845056 | tf_op jit(solution)/shard_map/dot_general | solution.py:106
  (53 shorter events, 39.7 us)
Async XLA Ops:
  6.5 115.7 %copy-start.2 = (f32[8192]{0:T(1024)S(1)}, f32[8192]{0:T(1024)}, u32[]{:S(2)}) copy-start(f32[8192]{0:T(1024)} %param.7) | copy-start | bytes 98308
  6.5 110.6 %all-gather.7.cloned.1.call-start = ((), (), s32[]{:S(2)}) async-start(), calls=%async_computation | async-start | bytes 8650752 | tf_op jit(solution)/shard_map/all_gather | solution.py:36
  7.3 146.8 %all-gather.11.cloned.1.call-start = ((), (), s32[]{:S(2)}) async-start(), calls=%async_computation.2 | async-start | bytes 4718592 | tf_op jit(solution)/shard_map/all_gather | solution.py:50
  8.2 4.9 %collective-permute-start = (bf16[1024,2,32]{0,2,1:T(8,128)(2,1)S(1)}, bf16[1024,2,32]{0,2,1:T(8,128)(2,1)S(1)}, u32[]{:S(2)}, u32[]{:S(2)}) collective-permute-start(bf16[1024,2,32]{0,2,1:T(8,128)(2,1)S(1)} %pad_maximum_fusion.2), channel_id=1, source_target_pairs={{0,1},{1,0},{2,3},{3,2},{4,5},{5,4},{6,7},{7,6},{8,9},{9,8},{10,11... | collective-permute-start | bytes 393224 | tf_op jit(solution)/shard_map/ppermute | solution.py:10
  14.0 15.2 %collective-permute-start.1 = (bf16[1024,2,64]{0,2,1:T(8,128)(2,1)S(1)}, bf16[1024,2,64]{0,2,1:T(8,128)(2,1)S(1)}, u32[]{:S(2)}, u32[]{:S(2)}) collective-permute-start(bf16[1024,2,64]{0,2,1:T(8,128)(2,1)S(1)} %pad_maximum_fusion.1), channel_id=1, source_target_pairs={{0,2},{1,3},{2,0},{3,1},{4,6},{5,7},{6,4},{7,5},{8,10},{9,11},{10,... | collective-permute-start | bytes 786440 | tf_op jit(solution)/shard_map/ppermute | solution.py:10
  29.4 8.9 %collective-permute-start.2 = (bf16[1024,2,128]{0,2,1:T(8,128)(2,1)S(1)}, bf16[1024,2,128]{0,2,1:T(8,128)(2,1)S(1)}, u32[]{:S(2)}, u32[]{:S(2)}) collective-permute-start(bf16[1024,2,128]{0,2,1:T(8,128)(2,1)S(1)} %pad_maximum_fusion), channel_id=1, source_target_pairs={{0,32},{32,64},{64,96},{96,128},{128,160},{160,192},{192,224},{224... | collective-permute-start | bytes 1572872 | tf_op jit(solution)/shard_map/ppermute | solution.py:56
  38.2 8.6 %collective-permute-start.3 = (bf16[1024,2,128]{0,2,1:T(8,128)(2,1)S(1)}, bf16[1024,2,128]{0,2,1:T(8,128)(2,1)S(1)}, u32[]{:S(2)}, u32[]{:S(2)}) collective-permute-start(bf16[1024,2,128]{0,2,1:T(8,128)(2,1)S(1)} %collective-permute-done.2), channel_id=1, source_target_pairs={{0,32},{32,64},{64,96},{96,128},{128,160},{160,192},{192,224},{224... | collective-permute-start | bytes 1572872 | tf_op jit(solution)/shard_map/ppermute | solution.py:56
  46.8 8.6 %collective-permute-start.4 = (bf16[1024,2,128]{0,2,1:T(8,128)(2,1)S(1)}, bf16[1024,2,128]{0,2,1:T(8,128)(2,1)S(1)}, u32[]{:S(2)}, u32[]{:S(2)}) collective-permute-start(bf16[1024,2,128]{0,2,1:T(8,128)(2,1)S(1)} %collective-permute-done.3), channel_id=1, source_target_pairs={{0,32},{32,64},{64,96},{96,128},{128,160},{160,192},{192,224},{224... | collective-permute-start | bytes 1572872 | tf_op jit(solution)/shard_map/ppermute | solution.py:56
  49.3 132.5 %all-gather.9.cloned.1.call-start = ((), (), s32[]{:S(2)}) async-start(), calls=%async_computation.1 | async-start | bytes 1179648 | tf_op jit(solution)/shard_map/all_gather | solution.py:78
  55.4 8.6 %collective-permute-start.5 = (bf16[1024,2,128]{0,2,1:T(8,128)(2,1)S(1)}, bf16[1024,2,128]{0,2,1:T(8,128)(2,1)S(1)}, u32[]{:S(2)}, u32[]{:S(2)}) collective-permute-start(bf16[1024,2,128]{0,2,1:T(8,128)(2,1)S(1)} %collective-permute-done.4), channel_id=1, source_target_pairs={{0,32},{32,64},{64,96},{96,128},{128,160},{160,192},{192,224},{224... | collective-permute-start | bytes 1572872 | tf_op jit(solution)/shard_map/ppermute | solution.py:56
  64.1 8.6 %collective-permute-start.6 = (bf16[1024,2,128]{0,2,1:T(8,128)(2,1)S(1)}, bf16[1024,2,128]{0,2,1:T(8,128)(2,1)}, u32[]{:S(2)}, u32[]{:S(2)}) collective-permute-start(bf16[1024,2,128]{0,2,1:T(8,128)(2,1)S(1)} %collective-permute-done.5), channel_id=1, source_target_pairs={{0,32},{32,64},{64,96},{96,128},{128,160},{160,192},{192,224},{224... | collective-permute-start | bytes 1572872 | tf_op jit(solution)/shard_map/ppermute | solution.py:56
  72.7 9.1 %collective-permute-start.7 = (bf16[1024,2,128]{0,2,1:T(8,128)(2,1)}, bf16[1024,2,128]{0,2,1:T(8,128)(2,1)S(1)}, u32[]{:S(2)}, u32[]{:S(2)}) collective-permute-start(bf16[1024,2,128]{0,2,1:T(8,128)(2,1)} %collective-permute-done.6), channel_id=1, source_target_pairs={{0,32},{32,64},{64,96},{96,128},{128,160},{160,192},{192,224},{224... | collective-permute-start | bytes 1572872 | tf_op jit(solution)/shard_map/ppermute | solution.py:56
  81.8 59.1 %collective-permute-start.8 = (bf16[1024,2,128]{0,2,1:T(8,128)(2,1)S(1)}, bf16[1024,2,128]{0,2,1:T(8,128)(2,1)}, u32[]{:S(2)}, u32[]{:S(2)}) collective-permute-start(bf16[1024,2,128]{0,2,1:T(8,128)(2,1)S(1)} %collective-permute-done.7), channel_id=1, source_target_pairs={{0,32},{32,64},{64,96},{96,128},{128,160},{160,192},{192,224},{224... | collective-permute-start | bytes 1572872 | tf_op jit(solution)/shard_map/ppermute | solution.py:56
  132.2 7.8 %copy-start = (bf16[512,8192]{1,0:T(8,128)(2,1)S(1)}, bf16[512,8192]{1,0:T(8,128)(2,1)}, u32[]{:S(2)}) copy-start(bf16[512,8192]{1,0:T(8,128)(2,1)} %fusion.2) | copy-start | bytes 25165828
  144.7 64.7 %all-gather.13.cloned.1.call-start = ((), (), s32[]{:S(2)}) async-start(), calls=%async_computation.3 | async-start | bytes 1179648 | tf_op jit(solution)/shard_map/all_gather | solution.py:79
  145.5 100.2 %all-gather.17.cloned.1.call-start = ((), (), s32[]{:S(2)}) async-start(), calls=%async_computation.5 | async-start | bytes 4718592 | tf_op jit(solution)/shard_map/all_gather | solution.py:107
  146.1 199.7 %all-gather.15.cloned.1.call-start = ((), (), s32[]{:S(2)}) async-start(), calls=%async_computation.4 | async-start | bytes 8650752 | tf_op jit(solution)/shard_map/all_gather | solution.py:104
  186.9 5.7 %copy-start.1 = (f32[4096,512,2]{1,0,2:T(8,128)}, f32[4096,512,2]{1,0,2:T(8,128)S(1)}, u32[]{:S(2)}) copy-start(f32[4096,512,2]{1,0,2:T(8,128)S(1)} %get-tuple-element.18) | copy-start | bytes 50331652
Sparse Core Ops, SparseCore 0:
  9.8 107.2 all-gather.6
  119.0 35.0 all-gather.10
  155.9 25.8 all-gather.8
  183.6 25.7 all-gather.12
  211.1 34.5 all-gather.16
  248.1 97.6 all-gather.14
